TPU v7x, 32 devices: a whole 2x2x4 slice. The times are simulated.
32 devices in a mesh: dp: 8 (over y, x, core), tensor: 4 (over z).
Axes of the slice: x: 2, y: 2, z: 4, core: 2. Of those that a mesh axis runs over, the one named last changes fastest.
Arguments:
- tokens: bfloat16 [16384, 768], P(('dp', 'tensor')), may hold values from -6 to 6
- starts: int32 [8, 8], P('dp'), may hold values from 0 to 2047, as said below
- w_qkv: bfloat16 [768, 2304], P(None, 'tensor'), may hold values from -0.21875 to 0.21875
- b_qkv: bfloat16 [2304], P('tensor'), may hold values from -3 to 3
- w_out: bfloat16 [768, 768], P('tensor'), may hold values from -2 to 2
- b_out: bfloat16 [768], replicated, may hold values from -3 to 3
- gain_one: bfloat16 [768], replicated, may hold values from 0.099609375 to 1.8984375
- shift_one: bfloat16 [768], replicated, may hold values from -3 to 3
- w_in: bfloat16 [768, 3072], P(None, 'tensor'), may hold values from -0.21875 to 0.21875
- b_in: bfloat16 [3072], P('tensor'), may hold values from -3 to 3
- w_two: bfloat16 [3072, 768], P('tensor'), may hold values from -0.21875 to 0.21875
- b_two: bfloat16 [768], replicated, may hold values from -3 to 3
- gain_two: bfloat16 [768], replicated, may hold values from 0.099609375 to 1.8984375
- shift_two: bfloat16 [768], replicated, may hold values from -3 to 3
- cotangent: bfloat16 [16384, 768], P(('dp', 'tensor')), may hold values from -6 to 6
Outputs:
- block_out: bfloat16 [16384, 768], P(('dp', 'tensor'))
- d_tokens: bfloat16 [16384, 768], P(('dp', 'tensor'))
- d_w_qkv: float32 [768, 2304], P(None, 'tensor')
- d_b_qkv: float32 [2304], P('tensor')
- d_w_out: float32 [768, 768], P('tensor')
- d_b_out: float32 [768], replicated
- d_gain_one: float32 [768], replicated
- d_shift_one: float32 [768], replicated
- d_w_in: float32 [768, 3072], P(None, 'tensor')
- d_b_in: float32 [3072], P('tensor')
- d_w_two: float32 [3072, 768], P('tensor')
- d_b_two: float32 [768], replicated
- d_gain_two: float32 [768], replicated
- d_shift_two: float32 [768], replicated
Inputs may be any that keep to these rules, and one draw needn't show every extreme that they name: Each row holds exactly 8 documents: its first start is 0 and its starts rise strictly. In the first row the last document is a single token.
All inputs are finite; a program needn't handle non-finite values.
Results may differ from a plain program's by a relative error of at most 0.014.
Values may be sent and summed in bfloat16 or wider, within the bound.
No kernel may reach another device: no remote copies, remote signals or barrier semaphores. Data moves between devices by JAX's collectives and lax.ppermute only.
A program may use at most 192 MiB of HBM per device.

v0:
```python
import math
import jax
import jax.numpy as jnp
from jax import lax
from jax.sharding import PartitionSpec as P

HEAD = 64
GROUP = 64
ROW_LEN = 2048
DOCS = 8
highest = lax.Precision.HIGHEST


def doc_tables(starts_row):
    places = jnp.arange(ROW_LEN, dtype=jnp.int32)
    started = (places[:, None] >= starts_row[None, :]).astype(jnp.int32)
    doc_ids = jnp.sum(started, axis=1) - 1
    onehot = (doc_ids[:, None] == jnp.arange(DOCS, dtype=jnp.int32)[None, :]).astype(jnp.int32)
    finish = jnp.concatenate([starts_row[1:], jnp.full((1,), ROW_LEN, jnp.int32)])
    own_start = jnp.sum(onehot * starts_row[None, :], axis=1)
    own_len = jnp.sum(onehot * (finish - starts_row)[None, :], axis=1)
    angles = 0.5 * math.pi * (places - own_start).astype(jnp.float32) / own_len.astype(jnp.float32)
    return (angles, doc_ids)


def attend(mixed, angles, doc_ids):
    length = mixed.shape[0]
    head_count = mixed.shape[1] // (3 * HEAD)
    blocks = length // GROUP
    pieces = mixed.reshape(blocks, GROUP, head_count, 3, HEAD)
    queries = jax.nn.relu(pieces[:, :, :, 0])
    key_pos = jax.nn.relu(pieces[:, :, :, 1])
    values = pieces[:, :, :, 2]
    cosine = jnp.cos(angles).reshape(blocks, GROUP, 1, 1)
    sines = jnp.sin(angles).reshape(blocks, GROUP, 1, 1)
    query_feat = jnp.concatenate([queries * cosine, queries * sines], axis=-1)
    key_feat = jnp.concatenate([key_pos * cosine, key_pos * sines], axis=-1)
    doc_blocks = doc_ids.reshape(blocks, GROUP)
    within = jnp.arange(GROUP, dtype=jnp.int32)
    inside_mask = (
        (doc_blocks[:, :, None] == doc_blocks[:, None, :])
        & (within[None, :, None] >= within[None, None, :])
    ).astype(jnp.float32)
    scores = (
        jnp.einsum("bihf,bjhf->bhij", query_feat, key_feat, precision=highest)
        * inside_mask[:, None]
    )
    numerator = jnp.einsum("bhij,bjhd->bihd", scores, values, precision=highest)
    denominator = jnp.transpose(jnp.sum(scores, axis=-1), (0, 2, 1))
    first_doc = doc_blocks[:, 0]
    last_doc = doc_blocks[:, -1]
    tail_mask = (doc_blocks == last_doc[:, None]).astype(jnp.float32)
    states = jnp.einsum("bjhf,bjhd,bj->bhfd", key_feat, values, tail_mask, precision=highest)
    key_sums = jnp.einsum("bjhf,bj->bhf", key_feat, tail_mask, precision=highest)
    order = jnp.arange(blocks, dtype=jnp.int32)
    link_mask = (
        (last_doc[None, :] == first_doc[:, None]) & (order[None, :] < order[:, None])
    ).astype(jnp.float32)
    carried = jnp.einsum("cb,bhfd->chfd", link_mask, states, precision=highest)
    carried_sum = jnp.einsum("cb,bhf->chf", link_mask, key_sums, precision=highest)
    opening = (doc_blocks == first_doc[:, None]).astype(jnp.float32)
    numerator = numerator + jnp.einsum(
        "bihf,bhfd,bi->bihd", query_feat, carried, opening, precision=highest
    )
    denominator = denominator + jnp.einsum(
        "bihf,bhf,bi->bih", query_feat, carried_sum, opening, precision=highest
    )
    result = numerator / jnp.maximum(denominator, 1.0)[..., None]
    return result.reshape(length, head_count * HEAD)


def attend_rows(mixed, angles, doc_ids):
    row_count = angles.shape[0]
    shaped = mixed.reshape(row_count, angles.shape[1], mixed.shape[1])
    return jax.vmap(attend)(shaped, angles, doc_ids).reshape(mixed.shape[0], -1)


def normalize(rows_in, gain, shift):
    centred = rows_in - jnp.mean(rows_in, axis=-1, keepdims=True)
    spread = jnp.mean(centred * centred, axis=-1, keepdims=True)
    return centred * lax.rsqrt(spread + 1e-05) * gain + shift


def smooth(values):
    return jax.nn.gelu(values)


def inner_rows(left, right):
    return lax.dot_general(
        left, right, (((0,), (0,)), ((), ())), preferred_element_type=jnp.float32
    )


def times_rows(left, right):
    return lax.dot_general(
        left, right, (((1,), (1,)), ((), ())), preferred_element_type=jnp.float32
    )


def rows_product(source, weight):
    return jnp.dot(source, weight, preferred_element_type=jnp.float32)


def rows_back(source, weight):
    return times_rows(source, weight)


def on_device(
    tokens,
    starts,
    w_qkv,
    b_qkv,
    w_out,
    b_out,
    gain_one,
    shift_one,
    w_in,
    b_in,
    w_two,
    b_two,
    gain_two,
    shift_two,
    cotangent,
):
    angles, doc_ids = jax.vmap(doc_tables)(starts)
    bias_qkv = b_qkv.astype(jnp.float32)
    bias_in = b_in.astype(jnp.float32)
    gain_a = gain_one.astype(jnp.float32)
    shift_a = shift_one.astype(jnp.float32)
    gain_b = gain_two.astype(jnp.float32)
    shift_b = shift_two.astype(jnp.float32)
    input_full = lax.all_gather(tokens, "tensor", axis=0, tiled=True)
    mixed = jnp.dot(input_full, w_qkv, preferred_element_type=jnp.float32) + bias_qkv
    attended = attend_rows(mixed, angles, doc_ids).astype(jnp.bfloat16)
    branch = lax.psum_scatter(
        rows_product(attended, w_out), "tensor", scatter_dimension=0, tiled=True
    ) + b_out.astype(jnp.float32)
    first_sum = tokens.astype(jnp.float32) + branch
    first_low = normalize(first_sum, gain_a, shift_a).astype(jnp.bfloat16)
    middle_full = lax.all_gather(first_low, "tensor", axis=0, tiled=True)
    hidden = jnp.dot(middle_full, w_in, preferred_element_type=jnp.float32) + bias_in
    active = smooth(hidden).astype(jnp.bfloat16)
    second = lax.psum_scatter(
        rows_product(active, w_two), "tensor", scatter_dimension=0, tiled=True
    ) + b_two.astype(jnp.float32)
    second_sum = first_low.astype(jnp.float32) + second
    block_out = normalize(second_sum, gain_b, shift_b).astype(jnp.bfloat16)
    input_back = lax.all_gather(tokens, "tensor", axis=0, tiled=True)
    middle_back = lax.all_gather(first_low, "tensor", axis=0, tiled=True)
    unused_two, norm_two_back = jax.vjp(normalize, second_sum, gain_b, shift_b)
    d_r2, d_gain_two, d_shift_two = norm_two_back(cotangent.astype(jnp.float32))
    d_second = d_r2.astype(jnp.bfloat16)
    d_b_two = jnp.sum(d_second, axis=0, dtype=jnp.float32)
    second_full = lax.all_gather(d_second, "tensor", axis=0, tiled=True)
    hidden_again = jnp.dot(middle_back, w_in, preferred_element_type=jnp.float32) + bias_in
    active_val, gelu_back = jax.vjp(smooth, hidden_again)
    active_again = active_val.astype(jnp.bfloat16)
    d_w_two = inner_rows(active_again, second_full)
    d_active = times_rows(second_full, w_two)
    d_hidden = gelu_back(d_active)[0].astype(jnp.bfloat16)
    d_b_in = jnp.sum(d_hidden, axis=0, dtype=jnp.float32)
    d_w_in = inner_rows(middle_back, d_hidden)
    d_first = (
        lax.psum_scatter(rows_back(d_hidden, w_in), "tensor", scatter_dimension=0, tiled=True)
        + d_r2
    )
    unused_one, norm_one_back = jax.vjp(normalize, first_sum, gain_a, shift_a)
    d_r1, d_gain_one, d_shift_one = norm_one_back(d_first)
    d_branch = d_r1.astype(jnp.bfloat16)
    d_b_out = jnp.sum(d_branch, axis=0, dtype=jnp.float32)
    branch_full = lax.all_gather(d_branch, "tensor", axis=0, tiled=True)
    mixed_again = jnp.dot(input_back, w_qkv, preferred_element_type=jnp.float32) + bias_qkv
    attended_val, attend_back = jax.vjp(
        lambda mixed_in: attend_rows(mixed_in, angles, doc_ids), mixed_again
    )
    attended_again = attended_val.astype(jnp.bfloat16)
    d_w_out = inner_rows(attended_again, branch_full)
    d_attended = times_rows(branch_full, w_out)
    d_mixed = attend_back(d_attended)[0].astype(jnp.bfloat16)
    d_b_qkv = jnp.sum(d_mixed, axis=0, dtype=jnp.float32)
    d_w_qkv = inner_rows(input_back, d_mixed)
    d_tokens = (
        lax.psum_scatter(
            rows_back(d_mixed, w_qkv).astype(jnp.bfloat16),
            "tensor",
            scatter_dimension=0,
            tiled=True,
        ).astype(jnp.float32)
        + d_r1
    ).astype(jnp.bfloat16)
    d_w_qkv, d_b_qkv, d_w_out, d_w_in, d_b_in, d_w_two = lax.psum(
        (d_w_qkv, d_b_qkv, d_w_out, d_w_in, d_b_in, d_w_two), "dp"
    )
    d_b_out, d_gain_one, d_shift_one, d_b_two, d_gain_two, d_shift_two = lax.psum(
        (d_b_out, d_gain_one, d_shift_one, d_b_two, d_gain_two, d_shift_two), ("dp", "tensor")
    )
    return (
        block_out,
        d_tokens,
        d_w_qkv,
        d_b_qkv,
        d_w_out,
        d_b_out,
        d_gain_one,
        d_shift_one,
        d_w_in,
        d_b_in,
        d_w_two,
        d_b_two,
        d_gain_two,
        d_shift_two,
    )


def solution(mesh):
    in_specs = (
        P(("dp", "tensor"), None),
        P("dp", None),
        P(None, "tensor"),
        P("tensor"),
        P("tensor", None),
        P(),
        P(),
        P(),
        P(None, "tensor"),
        P("tensor"),
        P("tensor", None),
        P(),
        P(),
        P(),
        P(("dp", "tensor"), None),
    )
    out_specs = (
        P(("dp", "tensor"), None),
        P(("dp", "tensor"), None),
        P(None, "tensor"),
        P("tensor"),
        P("tensor", None),
        P(),
        P(),
        P(),
        P(None, "tensor"),
        P("tensor"),
        P("tensor", None),
        P(),
        P(),
        P(),
    )
    return jax.shard_map(
        on_device, mesh=mesh, in_specs=in_specs, out_specs=out_specs, check_vma=False
    )
```

profile of v0, /device:TPU:0, one launch (start us, length us, event | category | flops | bytes accessed | tf_op | source)
XLA Modules:
  0.0 1038.7 jit_solution(10530214980209661449)
XLA Ops:
  12.7 63.1 %all-gather.5.cloned.1.call-done = bf16[2048,768]{1,0:T(8,128)(2,1)} async-done(((bf16[512,768]{1,0:T(8,128)(2,1)}), bf16[2048,768]{1,0:T(8,128)(2,1)}) %all-gather.5.cloned.1.call-update) | async-done | bytes 3145744 | tf_op jit(solution)/shard_map/all_gather | solution.py:132
  75.8 6.3 convolution_add_fusion
  82.2 8.7 reshape_reshape.3
  90.9 8.2 fusion.101
  110.8 5.1 bitcast_multiply_fusion.4
  123.8 6.0 fusion.31
  134.0 5.0 fusion.78
  139.0 5.4 multiply_reduce_fusion.1
  144.4 5.4 fusion.24
  150.5 9.1 divide_convert_fusion
  169.7 107.1 %reduce-scatter.5.cloned.1.call-done = f32[512,768]{1,0:T(8,128)} async-done(((f32[2048,768]{1,0:T(8,128)}), f32[512,768]{1,0:T(8,128)}) %reduce-scatter.5.cloned.1.call-update) | async-done | bytes 1572880 | tf_op jit(solution)/shard_map/reduce_scatter | solution.py:135
  280.2 64.1 %all-gather.7.cloned.1.call-done = bf16[2048,768]{1,0:T(8,128)(2,1)} async-done(((bf16[512,768]{1,0:T(8,128)(2,1)}), bf16[2048,768]{1,0:T(8,128)(2,1)}) %all-gather.7.cloned.1.call-update) | async-done | bytes 3145744 | tf_op jit(solution)/shard_map/all_gather | solution.py:140
  344.3 8.4 multiply_convert_fusion
  361.3 107.1 %reduce-scatter.7.cloned.1.call-done = f32[512,768]{1,0:T(8,128)} async-done(((f32[2048,768]{1,0:T(8,128)}), f32[512,768]{1,0:T(8,128)}) %reduce-scatter.7.cloned.1.call-update) | async-done | bytes 1572880 | tf_op jit(solution)/shard_map/reduce_scatter | solution.py:143
  476.5 64.1 %all-gather.9.cloned.1.call-done = bf16[2048,768]{1,0:T(8,128)(2,1)} async-done(((bf16[512,768]{1,0:T(8,128)(2,1)}), bf16[2048,768]{1,0:T(8,128)(2,1)}) %all-gather.9.cloned.1.call-update) | async-done | bytes 3145744 | tf_op jit(solution)/shard_map/all_gather | solution.py:154
  540.6 9.8 convert_reduce_fusion.1
  556.7 109.5 %reduce-scatter.9.cloned.1.call-done = f32[512,768]{1,0:T(8,128)} async-done(((f32[2048,768]{1,0:T(8,128)}), f32[512,768]{1,0:T(8,128)}) %reduce-scatter.9.cloned.1.call-update) | async-done | bytes 1572880 | tf_op jit(solution)/shard_map/reduce_scatter | solution.py:164
  673.7 63.5 %all-gather.11.cloned.1.call-done = bf16[2048,768]{1,0:T(8,128)(2,1)} async-done(((bf16[512,768]{1,0:T(8,128)(2,1)}), bf16[2048,768]{1,0:T(8,128)(2,1)}) %all-gather.11.cloned.1.call-update) | async-done | bytes 3145744 | tf_op jit(solution)/shard_map/all_gather | solution.py:171
  742.9 12.0 %fusion.21 = f32[32,3,64,64]{2,3,1,0:T(8,128)} fusion(f32[32,3,64,64]{2,3,1,0:T(8,128)} %copy-done.21, f32[32,64,64]{1,2,0:T(8,128)S(1)} %copy-done.12, f32[1,32,64,3,64]{2,1,4,3,0:T(8,128)} %reshape.798, f32[32,64,3]{1,2,0:T(4,128)S(1)} %copy-done.42), kind=kOutput, calls=%fused_computation.38 | convolution fusion | flops 302776320 | bytes 5267456 | tf_op jit(solution)/shard_map/transpose(jvp(vmap(bhij,bjhd->bihd)))/dot_general | solution.py:48
  754.9 7.4 fusion.19
  764.7 5.4 multiply_reduce_fusion
  777.2 8.3 fusion.42
  789.3 5.8 fusion.30
  795.2 7.7 fusion.13
  802.9 7.0 fusion.38
  814.7 8.1 add_bitcast_fusion
  828.5 7.4 copy.171
  835.9 6.7 convert_element_type.170
  847.0 7.1 fusion.108
  864.5 43.0 %all-reduce.3 = (f32[768]{0:T(1024)}, f32[768]{0:T(1024)}, f32[768]{0:T(1024)}, f32[768]{0:T(1024)}, f32[768]{0:T(1024)}, /*index=5*/f32[768]{0:T(1024)}) all-reduce(f32[768]{0:T(1024)S(1)} %copy-done.71, f32[768]{0:T(1024)S(1)} %copy-done.72, f32[768]{0:T(1024)S(1)} %copy-done.73, ...), channel_id=1, replica_groups=mesh['dp'=8,'tensor'=4] {'dp','tensor'}, use_global_device_ids=true, to_apply=%region_22.23 | all-reduce | flops 4608 | bytes 36864 | tf_op jit(solution)/shard_map/psum | solution.py:194
  907.5 14.0 %all-reduce.4 = (f32[576]{0:T(1024)}, f32[768]{0:T(1024)}) all-reduce(f32[576]{0:T(1024)S(1)} %reduce_sum.223, f32[768]{0:T(1024)S(1)} %copy-done.76), channel_id=1, replica_groups=mesh['dp'=8,'tensor'=4] {'dp'}, use_global_device_ids=true, to_apply=%region_19.20 | all-reduce | flops 1344 | bytes 10752 | tf_op jit(solution)/shard_map/psum | solution.py:191
  923.8 101.3 %all-reduce.8.cloned.1.call-done = (f32[768,576]{0,1:T(8,128)}, f32[192,768]{1,0:T(8,128)}, f32[768,768]{1,0:T(8,128)}, f32[768,768]{1,0:T(8,128)}) async-done(((f32[768,576]{0,1:T(8,128)}, f32[192,768]{1,0:T(8,128)}, f32[768,768]{1,0:T(8,128)}, f32[768,768]{1,0:T(8,128)}), (f32[768,576]{0,1:T(8,128)}, f32[192,768]{1,0:T(8,128)}, f32[768,768]{1,0:T(8,128)}, ...) | async-done | bytes 7077904 | tf_op jit(solution)/shard_map/psum | solution.py:191
  (281 shorter events, 126.3 us)
Async XLA Ops:
  7.2 337.2 %copy-start = (bf16[768,768]{1,0:T(8,128)(2,1)S(1)}, bf16[768,768]{1,0:T(8,128)(2,1)}, u32[]{:S(2)}) copy-start(bf16[768,768]{1,0:T(8,128)(2,1)} %param.23) | copy-start | bytes 3538948
  7.2 68.6 %all-gather.5.cloned.1.call-start = ((), (), s32[]{:S(2)}) async-start(), calls=%async_computation.4 | async-start | bytes 3932160 | tf_op jit(solution)/shard_map/all_gather | solution.py:132
  7.9 268.9 %reduce-scatter.5.cloned.1.call-start = ((), (), s32[]{:S(2)}) async-start(), calls=%async_computation.5 | async-start | bytes 7864320 | tf_op jit(solution)/shard_map/reduce_scatter | solution.py:135
  12.1 117.7 %copy-start.61 = (s32[32]{0:T(128)}, s32[32]{0:T(128)S(1)}, u32[]{:S(2)}) copy-start(s32[32]{0:T(128)S(1)} %get-tuple-element.20) | copy-start | bytes 388
  12.1 117.7 %copy-start.64 = (s32[32]{0:T(128)}, s32[32]{0:T(128)S(1)}, u32[]{:S(2)}) copy-start(s32[32]{0:T(128)S(1)} %get-tuple-element.21) | copy-start | bytes 388
  12.2 109.0 %copy-start.39 = (f32[32,64]{1,0:T(8,128)}, f32[32,64]{1,0:T(8,128)S(1)}, u32[]{:S(2)}) copy-start(f32[32,64]{1,0:T(8,128)S(1)} %get-tuple-element.57) | copy-start | bytes 24580
  12.3 98.5 %copy-start.44 = (f32[32,64]{1,0:T(8,128)}, f32[32,64]{1,0:T(8,128)S(1)}, u32[]{:S(2)}) copy-start(f32[32,64]{1,0:T(8,128)S(1)} %get-tuple-element.71) | copy-start | bytes 24580
  12.3 98.4 %copy-start.46 = (f32[32,64]{1,0:T(8,128)}, f32[32,64]{1,0:T(8,128)S(1)}, u32[]{:S(2)}) copy-start(f32[32,64]{1,0:T(8,128)S(1)} %get-tuple-element.72) | copy-start | bytes 24580
  12.7 131.7 %copy-start.11 = (f32[32,64,64]{1,2,0:T(8,128)}, f32[32,64,64]{1,2,0:T(8,128)S(1)}, u32[]{:S(2)}) copy-start(f32[32,64,64]{1,2,0:T(8,128)S(1)} %and_convert_fusion) | copy-start | bytes 1572868
  167.2 109.6 %copy-start.27 = (bf16[512,768]{1,0:T(8,128)(2,1)S(1)}, bf16[512,768]{1,0:T(8,128)(2,1)}, u32[]{:S(2)}) copy-start(bf16[512,768]{1,0:T(8,128)(2,1)} %param.15) | copy-start | bytes 2359300
  167.3 177.1 %all-gather.7.cloned.1.call-start = ((), (), s32[]{:S(2)}) async-start(), calls=%async_computation.6 | async-start | bytes 3932160 | tf_op jit(solution)/shard_map/all_gather | solution.py:140
  278.6 74.1 %copy-start.50 = (f32[512]{0:T(512)}, f32[512]{0:T(512)S(1)}, u32[]{:S(2)}) copy-start(f32[512]{0:T(512)S(1)} %broadcast_multiply_fusion.1) | copy-start | bytes 6148
  278.9 73.8 %copy-start.57 = (f32[512]{0:T(512)}, f32[512]{0:T(512)S(1)}, u32[]{:S(2)}) copy-start(f32[512]{0:T(512)S(1)} %multiply_reduce_fusion.5) | copy-start | bytes 6148
  278.9 73.8 %copy-start.53 = (f32[512]{0:T(512)}, f32[512]{0:T(512)S(1)}, u32[]{:S(2)}) copy-start(f32[512]{0:T(512)S(1)} %fusion.86) | copy-start | bytes 6148
  280.2 188.3 %reduce-scatter.7.cloned.1.call-start = ((), (), s32[]{:S(2)}) async-start(), calls=%async_computation.7 | async-start | bytes 7864320 | tf_op jit(solution)/shard_map/reduce_scatter | solution.py:143
  280.2 72.5 %copy-start.74 = (f32[768]{0:T(1024)}, f32[768]{0:T(1024)S(1)}, u32[]{:S(2)}) copy-start(f32[768]{0:T(1024)S(1)} %convert_element_type.159) | copy-start | bytes 9220
  358.9 181.8 %all-gather.9.cloned.1.call-start = ((), (), s32[]{:S(2)}) async-start(), calls=%async_computation.8 | async-start | bytes 3932160 | tf_op jit(solution)/shard_map/all_gather | solution.py:154
  361.3 109.5 %copy-start.26 = (bf16[512,768]{1,0:T(8,128)(2,1)S(1)}, bf16[512,768]{1,0:T(8,128)(2,1)}, u32[]{:S(2)}) copy-start(bf16[512,768]{1,0:T(8,128)(2,1)} %param.29) | copy-start | bytes 2359300
  473.6 67.0 %copy-start.75 = (f32[768]{0:T(1024)S(1)}, f32[768]{0:T(1024)}, u32[]{:S(2)}) copy-start(f32[768]{0:T(1024)} %copy-done.74) | copy-start | bytes 9220
  476.4 189.7 %reduce-scatter.9.cloned.1.call-start = ((), (), s32[]{:S(2)}) async-start(), calls=%async_computation.9 | async-start | bytes 7864320 | tf_op jit(solution)/shard_map/reduce_scatter | solution.py:164
  556.6 109.6 %copy-start.49 = (f32[768]{0:T(1024)S(1)}, f32[768]{0:T(1024)}, u32[]{:S(2)}) copy-start(f32[768]{0:T(1024)} %convert_element_type.155) | copy-start | bytes 9220
  556.6 109.6 %copy-start.51 = (f32[512]{0:T(512)S(1)}, f32[512]{0:T(512)}, u32[]{:S(2)}) copy-start(f32[512]{0:T(512)} %copy-done.50) | copy-start | bytes 6148
  556.6 109.6 %copy-start.54 = (f32[512]{0:T(512)S(1)}, f32[512]{0:T(512)}, u32[]{:S(2)}) copy-start(f32[512]{0:T(512)} %copy-done.53) | copy-start | bytes 6148
  556.6 112.9 %copy-start.58 = (f32[512]{0:T(512)S(1)}, f32[512]{0:T(512)}, u32[]{:S(2)}) copy-start(f32[512]{0:T(512)} %copy-done.57) | copy-start | bytes 6148
  556.6 180.5 %all-gather.11.cloned.1.call-start = ((), (), s32[]{:S(2)}) async-start(), calls=%async_computation.10 | async-start | bytes 3932160 | tf_op jit(solution)/shard_map/all_gather | solution.py:171
  669.5 67.7 %copy-start.31 = (bf16[192,768]{1,0:T(8,128)(2,1)S(1)}, bf16[192,768]{1,0:T(8,128)(2,1)}, u32[]{:S(2)}) copy-start(bf16[192,768]{1,0:T(8,128)(2,1)} %param.19) | copy-start | bytes 884740
  670.2 70.1 %copy-start.59 = (f32[512]{0:T(512)}, f32[512]{0:T(512)S(1)}, u32[]{:S(2)}) copy-start(f32[512]{0:T(512)S(1)} %negate_multiply_fusion) | copy-start | bytes 6148
  673.0 248.5 %reduce-scatter.11.cloned.1.call-start = ((), (), s32[]{:S(2)}) async-start(), calls=%async_computation.11 | async-start | bytes 3932160 | tf_op jit(solution)/shard_map/reduce_scatter | solution.py:183
  846.7 178.4 %all-reduce.8.cloned.1.call-start = ((), (), s32[]{:S(2)}) async-start(), calls=%async_computation.12 | async-start | bytes 14155776 | tf_op jit(solution)/shard_map/psum | solution.py:191
  863.7 43.8 %copy-start.76 = (f32[768]{0:T(1024)S(1)}, f32[768]{0:T(1024)}, u32[]{:S(2)}) copy-start(f32[768]{0:T(1024)} %get-tuple-element.40) | copy-start | bytes 9220
  863.7 57.8 %copy-start.16 = (f32[512,768]{1,0:T(8,128)S(1)}, f32[512,768]{1,0:T(8,128)}, u32[]{:S(2)}) copy-start(f32[512,768]{1,0:T(8,128)} %copy-done.15) | copy-start | bytes 4718596
  863.7 57.8 %copy-start.60 = (f32[512]{0:T(512)S(1)}, f32[512]{0:T(512)}, u32[]{:S(2)}) copy-start(f32[512]{0:T(512)} %copy-done.59) | copy-start | bytes 6148
  (68 other events, 355.0 us)
Sparse Core Ops, SparseCore 0:
  9.6 66.1 all-gather.4
  167.4 109.3 reduce-scatter.4
  280.3 64.0 all-gather.6
  359.0 109.3 reduce-scatter.6
  476.6 64.0 all-gather.8
  556.7 109.3 reduce-scatter.8
  673.1 64.0 all-gather.10
  846.8 59.8 reduce-scatter.10
  911.5 113.5 all-reduce.7
where the time goes:
time: 1050 us; the launch traced here: 1040 us
  waiting for transfers between devices  681 us (65%)
  matrix products  166 us (16%)
  local copies, waits for them, and re-layouts  73.7 us (7%)
  blocking collectives  57 us (5%)
  other arithmetic  45.5 us (4%)
  between operations  15.3 us (1%)
    reduce_scatter x1, waiting for transfers between devices, on_device(): lax.psum_scatter(rows_back(d_hidden, w_in), 'tensor', scatter_dimension=0...  109 us
    reduce_scatter x1, waiting for transfers between devices, on_device(): lax.psum_scatter(rows_product(attended, w_out), 'tensor', scatter_dimensi...  107 us
    reduce_scatter x1, waiting for transfers between devices, on_device(): lax.psum_scatter(rows_product(active, w_two), 'tensor', scatter_dimension...  107 us
    psum x1, waiting for transfers between devices, on_device(): lax.psum((d_w_qkv, d_b_qkv, d_w_out, d_w_in, d_b_in, d_w_two), 'dp')  101 us
    all_gather x1, waiting for transfers between devices, on_device(): second_full = lax.all_gather(d_second, 'tensor', axis=0, tiled=True)  64.1 us
    all_gather x1, waiting for transfers between devices, on_device(): middle_full = lax.all_gather(first_low, 'tensor', axis=0, tiled=True)  64.1 us
    all_gather x1, waiting for transfers between devices, on_device(): branch_full = lax.all_gather(d_branch, 'tensor', axis=0, tiled=True)  63.5 us
    all_gather x1, waiting for transfers between devices, on_device(): input_full = lax.all_gather(tokens, 'tensor', axis=0, tiled=True)  63.1 us
  transfers between devices with their start and end apart: 9, of which 8 were waited for; matrix products, arithmetic and copies ran while one was open for 3% of the time, Pallas kernels for 0%

commit v1 on v0

--- a/solution.py
+++ b/solution.py
@@ -146,12 +146,17 @@
     second_sum = first_low.astype(jnp.float32) + second
     block_out = normalize(second_sum, gain_b, shift_b).astype(jnp.bfloat16)
     input_back = lax.all_gather(tokens, "tensor", axis=0, tiled=True)
-    middle_back = lax.all_gather(first_low, "tensor", axis=0, tiled=True)
     unused_two, norm_two_back = jax.vjp(normalize, second_sum, gain_b, shift_b)
     d_r2, d_gain_two, d_shift_two = norm_two_back(cotangent.astype(jnp.float32))
     d_second = d_r2.astype(jnp.bfloat16)
     d_b_two = jnp.sum(d_second, axis=0, dtype=jnp.float32)
-    second_full = lax.all_gather(d_second, "tensor", axis=0, tiled=True)
+    middle_back, second_full = jnp.split(
+        lax.all_gather(
+            jnp.concatenate([first_low, d_second], axis=1), "tensor", axis=0, tiled=True
+        ),
+        [first_low.shape[1]],
+        axis=1,
+    )
     hidden_again = jnp.dot(middle_back, w_in, preferred_element_type=jnp.float32) + bias_in
     active_val, gelu_back = jax.vjp(smooth, hidden_again)
     active_again = active_val.astype(jnp.bfloat16)

time: 1050 us -> 1090 us (1.038)
  waiting for transfers between devices: 681 us -> 728 us
    all_gather x1, waiting for transfers between devices: 64.1 us -> 116 us  [on_device(): lax.all_gather(jnp.concatenate([first_low, d_second], axis=1), 'tensor',...]
    unnamed x189 -> x191, local copies, waits for them, and re-layouts: 29.2 us -> 27.7 us
where the time goes in v1:
time: 1090 us
  waiting for transfers between devices  728 us (67%)
  matrix products  169 us (16%)
  local copies, waits for them, and re-layouts  72.2 us (7%)
  blocking collectives  57.1 us (5%)
  other arithmetic  45.9 us (4%)
  between operations  15.4 us (1%)
    all_gather x1, waiting for transfers between devices, on_device(): lax.all_gather(jnp.concatenate([first_low, d_second], axis=1), 'tensor',...  116 us
    reduce_scatter x1, waiting for transfers between devices, on_device(): lax.psum_scatter(rows_back(d_hidden, w_in), 'tensor', scatter_dimension=0...  109 us
    reduce_scatter x1, waiting for transfers between devices, on_device(): lax.psum_scatter(rows_product(active, w_two), 'tensor', scatter_dimension...  107 us
    reduce_scatter x1, waiting for transfers between devices, on_device(): lax.psum_scatter(rows_product(attended, w_out), 'tensor', scatter_dimensi...  107 us
    psum x1, waiting for transfers between devices, on_device(): lax.psum((d_w_qkv, d_b_qkv, d_w_out, d_w_in, d_b_in, d_w_two), 'dp')  96.9 us
    all_gather x1, waiting for transfers between devices, on_device(): middle_full = lax.all_gather(first_low, 'tensor', axis=0, tiled=True)  64.1 us
    all_gather x1, waiting for transfers between devices, on_device(): branch_full = lax.all_gather(d_branch, 'tensor', axis=0, tiled=True)  63.5 us
    all_gather x1, waiting for transfers between devices, on_device(): input_full = lax.all_gather(tokens, 'tensor', axis=0, tiled=True)  63.1 us
  transfers between devices with their start and end apart: 9, of which 8 were waited for; matrix products, arithmetic and copies ran while one was open for 3% of the time, Pallas kernels for 0%

profile of v1, /device:TPU:0, one launch (start us, length us, event | category | flops | bytes accessed | tf_op | source)
XLA Modules:
  0.0 1087.9 jit_solution(12424413140488585899)
XLA Ops:
  12.7 63.1 %all-gather.5.cloned.1.call-done = bf16[2048,768]{1,0:T(8,128)(2,1)} async-done(((bf16[512,768]{1,0:T(8,128)(2,1)}), bf16[2048,768]{1,0:T(8,128)(2,1)}) %all-gather.5.cloned.1.call-update) | async-done | bytes 3145744 | tf_op jit(solution)/shard_map/all_gather | solution.py:132
  75.8 6.3 convolution_add_fusion
  82.2 8.7 reshape_reshape.3
  90.9 8.1 fusion.127
  110.8 5.0 bitcast_multiply_fusion.4
  123.8 6.0 fusion.40
  138.9 5.4 multiply_reduce_fusion.1
  144.3 5.4 fusion.32
  150.5 9.2 divide_convert_fusion
  169.7 107.1 %reduce-scatter.5.cloned.1.call-done = f32[512,768]{1,0:T(8,128)} async-done(((f32[2048,768]{1,0:T(8,128)}), f32[512,768]{1,0:T(8,128)}) %reduce-scatter.5.cloned.1.call-update) | async-done | bytes 1572880 | tf_op jit(solution)/shard_map/reduce_scatter | solution.py:135
  280.2 64.1 %all-gather.7.cloned.1.call-done = bf16[2048,768]{1,0:T(8,128)(2,1)} async-done(((bf16[512,768]{1,0:T(8,128)(2,1)}), bf16[2048,768]{1,0:T(8,128)(2,1)}) %all-gather.7.cloned.1.call-update) | async-done | bytes 3145744 | tf_op jit(solution)/shard_map/all_gather | solution.py:140
  344.3 9.4 fusion.86
  356.3 107.1 %reduce-scatter.7.cloned.1.call-done = f32[512,768]{1,0:T(8,128)} async-done(((f32[2048,768]{1,0:T(8,128)}), f32[512,768]{1,0:T(8,128)}) %reduce-scatter.7.cloned.1.call-update) | async-done | bytes 1572880 | tf_op jit(solution)/shard_map/reduce_scatter | solution.py:143
  471.9 116.0 %all-gather.9.cloned.1.call-done = bf16[2048,1536]{1,0:T(8,128)(2,1)} async-done(((bf16[512,1536]{1,0:T(8,128)(2,1)}), bf16[2048,1536]{1,0:T(8,128)(2,1)}) %all-gather.9.cloned.1.call-update) | async-done | bytes 6291472 | tf_op jit(solution)/shard_map/all_gather | solution.py:154
  592.6 7.1 convert_reduce_fusion.1
  606.1 109.1 %reduce-scatter.9.cloned.1.call-done = f32[512,768]{1,0:T(8,128)} async-done(((f32[2048,768]{1,0:T(8,128)}), f32[512,768]{1,0:T(8,128)}) %reduce-scatter.9.cloned.1.call-update) | async-done | bytes 1572880 | tf_op jit(solution)/shard_map/reduce_scatter | solution.py:169
  722.7 63.5 %all-gather.11.cloned.1.call-done = bf16[2048,768]{1,0:T(8,128)(2,1)} async-done(((bf16[512,768]{1,0:T(8,128)(2,1)}), bf16[2048,768]{1,0:T(8,128)(2,1)}) %all-gather.11.cloned.1.call-update) | async-done | bytes 3145744 | tf_op jit(solution)/shard_map/all_gather | solution.py:176
  791.9 12.0 %fusion.29 = f32[32,3,64,64]{2,3,1,0:T(8,128)} fusion(f32[32,3,64,64]{2,3,1,0:T(8,128)} %copy-done.21, f32[32,64,64]{1,2,0:T(8,128)S(1)} %copy-done.12, f32[1,32,64,3,64]{2,1,4,3,0:T(8,128)} %reshape.798, f32[32,64,3]{1,2,0:T(4,128)S(1)} %copy-done.43), kind=kOutput, calls=%fused_computation.47 | convolution fusion | flops 302776320 | bytes 5267456 | tf_op jit(solution)/shard_map/transpose(jvp(vmap(bhij,bjhd->bihd)))/dot_general | solution.py:48
  803.9 7.3 fusion.27
  813.6 5.4 multiply_reduce_fusion
  826.0 8.3 fusion.60
  838.1 5.8 fusion.39
  844.0 7.7 fusion.21
  851.8 7.1 fusion.47
  863.7 8.1 add_bitcast_fusion
  877.5 7.4 copy.171
  884.9 6.7 convert_element_type.172
  896.0 7.0 fusion.49
  903.1 8.7 fusion.38
  918.0 42.7 %all-reduce.3 = (f32[768]{0:T(1024)}, f32[768]{0:T(1024)}, f32[768]{0:T(1024)}, f32[768]{0:T(1024)}, f32[768]{0:T(1024)}, /*index=5*/f32[768]{0:T(1024)}) all-reduce(f32[768]{0:T(1024)S(1)} %copy-done.72, f32[768]{0:T(1024)S(1)} %copy-done.73, f32[768]{0:T(1024)S(1)} %copy-done.74, ...), channel_id=1, replica_groups=mesh['dp'=8,'tensor'=4] {'dp','tensor'}, use_global_device_ids=true, to_apply=%region_22.23 | all-reduce | flops 4608 | bytes 36864 | tf_op jit(solution)/shard_map/psum | solution.py:199
  960.8 14.3 %all-reduce.4 = (f32[576]{0:T(1024)}, f32[768]{0:T(1024)}) all-reduce(f32[576]{0:T(1024)S(1)} %reduce_sum.223, f32[768]{0:T(1024)S(1)} %copy-done.78), channel_id=1, replica_groups=mesh['dp'=8,'tensor'=4] {'dp'}, use_global_device_ids=true, to_apply=%region_19.20 | all-reduce | flops 1344 | bytes 10752 | tf_op jit(solution)/shard_map/psum | solution.py:196
  977.4 96.9 %all-reduce.8.cloned.1.call-done = (f32[768,576]{0,1:T(8,128)}, f32[192,768]{1,0:T(8,128)}, f32[768,768]{1,0:T(8,128)}, f32[768,768]{1,0:T(8,128)}) async-done(((f32[768,576]{0,1:T(8,128)}, f32[192,768]{1,0:T(8,128)}, f32[768,768]{1,0:T(8,128)}, f32[768,768]{1,0:T(8,128)}), (f32[768,576]{0,1:T(8,128)}, f32[192,768]{1,0:T(8,128)}, f32[768,768]{1,0:T(8,128)}, ...) | async-done | bytes 7077904 | tf_op jit(solution)/shard_map/psum | solution.py:196
  (284 shorter events, 126.3 us)
Async XLA Ops:
  7.2 337.1 %copy-start = (bf16[768,768]{1,0:T(8,128)(2,1)S(1)}, bf16[768,768]{1,0:T(8,128)(2,1)}, u32[]{:S(2)}) copy-start(bf16[768,768]{1,0:T(8,128)(2,1)} %param.23) | copy-start | bytes 3538948
  7.2 68.6 %all-gather.5.cloned.1.call-start = ((), (), s32[]{:S(2)}) async-start(), calls=%async_computation.4 | async-start | bytes 3932160 | tf_op jit(solution)/shard_map/all_gather | solution.py:132
  7.9 268.9 %reduce-scatter.5.cloned.1.call-start = ((), (), s32[]{:S(2)}) async-start(), calls=%async_computation.5 | async-start | bytes 7864320 | tf_op jit(solution)/shard_map/reduce_scatter | solution.py:135
  12.1 117.7 %copy-start.62 = (s32[32]{0:T(128)}, s32[32]{0:T(128)S(1)}, u32[]{:S(2)}) copy-start(s32[32]{0:T(128)S(1)} %get-tuple-element.20) | copy-start | bytes 388
  12.1 117.7 %copy-start.65 = (s32[32]{0:T(128)}, s32[32]{0:T(128)S(1)}, u32[]{:S(2)}) copy-start(s32[32]{0:T(128)S(1)} %get-tuple-element.21) | copy-start | bytes 388
  12.2 109.0 %copy-start.40 = (f32[32,64]{1,0:T(8,128)}, f32[32,64]{1,0:T(8,128)S(1)}, u32[]{:S(2)}) copy-start(f32[32,64]{1,0:T(8,128)S(1)} %get-tuple-element.55) | copy-start | bytes 24580
  12.3 98.5 %copy-start.45 = (f32[32,64]{1,0:T(8,128)}, f32[32,64]{1,0:T(8,128)S(1)}, u32[]{:S(2)}) copy-start(f32[32,64]{1,0:T(8,128)S(1)} %get-tuple-element.69) | copy-start | bytes 24580
  12.3 98.5 %copy-start.47 = (f32[32,64]{1,0:T(8,128)}, f32[32,64]{1,0:T(8,128)S(1)}, u32[]{:S(2)}) copy-start(f32[32,64]{1,0:T(8,128)S(1)} %get-tuple-element.70) | copy-start | bytes 24580
  12.7 131.6 %copy-start.11 = (f32[32,64,64]{1,2,0:T(8,128)}, f32[32,64,64]{1,2,0:T(8,128)S(1)}, u32[]{:S(2)}) copy-start(f32[32,64,64]{1,2,0:T(8,128)S(1)} %and_convert_fusion) | copy-start | bytes 1572868
  167.2 109.6 %copy-start.28 = (bf16[512,768]{1,0:T(8,128)(2,1)S(1)}, bf16[512,768]{1,0:T(8,128)(2,1)}, u32[]{:S(2)}) copy-start(bf16[512,768]{1,0:T(8,128)(2,1)} %param.15) | copy-start | bytes 2359300
  167.3 177.1 %all-gather.7.cloned.1.call-start = ((), (), s32[]{:S(2)}) async-start(), calls=%async_computation.6 | async-start | bytes 3932160 | tf_op jit(solution)/shard_map/all_gather | solution.py:140
  278.5 75.2 %copy-start.51 = (f32[512]{0:T(512)}, f32[512]{0:T(512)S(1)}, u32[]{:S(2)}) copy-start(f32[512]{0:T(512)S(1)} %broadcast_multiply_fusion.1) | copy-start | bytes 6148
  278.9 74.9 %copy-start.58 = (f32[512]{0:T(512)}, f32[512]{0:T(512)S(1)}, u32[]{:S(2)}) copy-start(f32[512]{0:T(512)S(1)} %multiply_reduce_fusion.5) | copy-start | bytes 6148
  278.9 74.9 %copy-start.54 = (f32[512]{0:T(512)}, f32[512]{0:T(512)S(1)}, u32[]{:S(2)}) copy-start(f32[512]{0:T(512)S(1)} %fusion.105) | copy-start | bytes 6148
  280.1 183.3 %reduce-scatter.7.cloned.1.call-start = ((), (), s32[]{:S(2)}) async-start(), calls=%async_computation.7 | async-start | bytes 7864320 | tf_op jit(solution)/shard_map/reduce_scatter | solution.py:143
  280.2 73.6 %copy-start.75 = (f32[768]{0:T(1024)}, f32[768]{0:T(1024)S(1)}, u32[]{:S(2)}) copy-start(f32[768]{0:T(1024)S(1)} %convert_element_type.161) | copy-start | bytes 9220
  353.8 234.0 %all-gather.9.cloned.1.call-start = ((), (), s32[]{:S(2)}) async-start(), calls=%async_computation.8 | async-start | bytes 7864320 | tf_op jit(solution)/shard_map/all_gather | solution.py:154
  356.3 109.5 %copy-start.27 = (bf16[512,768]{1,0:T(8,128)(2,1)S(1)}, bf16[512,768]{1,0:T(8,128)(2,1)}, u32[]{:S(2)}) copy-start(bf16[512,768]{1,0:T(8,128)(2,1)} %param.29) | copy-start | bytes 2359300
  471.8 120.8 %copy-start.76 = (f32[768]{0:T(1024)S(1)}, f32[768]{0:T(1024)}, u32[]{:S(2)}) copy-start(f32[768]{0:T(1024)} %copy-done.75) | copy-start | bytes 9220
  471.8 243.3 %reduce-scatter.9.cloned.1.call-start = ((), (), s32[]{:S(2)}) async-start(), calls=%async_computation.9 | async-start | bytes 7864320 | tf_op jit(solution)/shard_map/reduce_scatter | solution.py:169
  606.0 109.2 %copy-start.50 = (f32[768]{0:T(1024)S(1)}, f32[768]{0:T(1024)}, u32[]{:S(2)}) copy-start(f32[768]{0:T(1024)} %convert_element_type.157) | copy-start | bytes 9220
  606.0 109.2 %copy-start.52 = (f32[512]{0:T(512)S(1)}, f32[512]{0:T(512)}, u32[]{:S(2)}) copy-start(f32[512]{0:T(512)} %copy-done.51) | copy-start | bytes 6148
  606.0 109.2 %copy-start.55 = (f32[512]{0:T(512)S(1)}, f32[512]{0:T(512)}, u32[]{:S(2)}) copy-start(f32[512]{0:T(512)} %copy-done.54) | copy-start | bytes 6148
  606.0 112.4 %copy-start.59 = (f32[512]{0:T(512)S(1)}, f32[512]{0:T(512)}, u32[]{:S(2)}) copy-start(f32[512]{0:T(512)} %copy-done.58) | copy-start | bytes 6148
  606.0 180.1 %all-gather.11.cloned.1.call-start = ((), (), s32[]{:S(2)}) async-start(), calls=%async_computation.10 | async-start | bytes 3932160 | tf_op jit(solution)/shard_map/all_gather | solution.py:176
  718.5 67.7 %copy-start.32 = (bf16[192,768]{1,0:T(8,128)(2,1)S(1)}, bf16[192,768]{1,0:T(8,128)(2,1)}, u32[]{:S(2)}) copy-start(bf16[192,768]{1,0:T(8,128)(2,1)} %param.19) | copy-start | bytes 884740
  719.1 70.1 %copy-start.60 = (f32[512]{0:T(512)}, f32[512]{0:T(512)S(1)}, u32[]{:S(2)}) copy-start(f32[512]{0:T(512)S(1)} %negate_multiply_fusion) | copy-start | bytes 6148
  722.0 253.2 %reduce-scatter.11.cloned.1.call-start = ((), (), s32[]{:S(2)}) async-start(), calls=%async_computation.11 | async-start | bytes 3932160 | tf_op jit(solution)/shard_map/reduce_scatter | solution.py:188
  895.7 178.6 %all-reduce.8.cloned.1.call-start = ((), (), s32[]{:S(2)}) async-start(), calls=%async_computation.12 | async-start | bytes 14155776 | tf_op jit(solution)/shard_map/psum | solution.py:196
  917.2 43.5 %copy-start.78 = (f32[768]{0:T(1024)S(1)}, f32[768]{0:T(1024)}, u32[]{:S(2)}) copy-start(f32[768]{0:T(1024)} %get-tuple-element.76) | copy-start | bytes 9220
  917.3 57.9 %copy-start.16 = (f32[512,768]{1,0:T(8,128)S(1)}, f32[512,768]{1,0:T(8,128)}, u32[]{:S(2)}) copy-start(f32[512,768]{1,0:T(8,128)} %copy-done.15) | copy-start | bytes 4718596
  917.3 57.9 %copy-start.61 = (f32[512]{0:T(512)S(1)}, f32[512]{0:T(512)}, u32[]{:S(2)}) copy-start(f32[512]{0:T(512)} %copy-done.60) | copy-start | bytes 6148
  (69 other events, 365.9 us)
Sparse Core Ops, SparseCore 0:
  9.6 66.1 all-gather.4
  167.4 109.3 reduce-scatter.4
  280.2 64.0 all-gather.6
  354.0 109.3 reduce-scatter.6
  471.9 115.8 all-gather.8
  606.1 108.9 reduce-scatter.8
  722.1 64.0 all-gather.10
  895.8 59.8 reduce-scatter.10
  960.5 113.7 all-reduce.7
